TPU v7x, 256 devices: a whole 4x4x8 slice. The times are simulated.
256 devices in a mesh: ha: 16 (over x, y_lo, core), wa: 16 (over z, y_hi).
Axes of the slice: x: 4, y: 4 (y_hi: 2, y_lo: 2; y = y_hi * 2 + y_lo), z: 8, core: 2. Of those that a mesh axis runs over, the one named last changes fastest.
Arguments:
- token_queries: bfloat16 [16, 4, 64, 64, 128], P(None, None, 'ha', 'wa'), may hold values from -48 to 48
- token_keys: bfloat16 [16, 4, 64, 64, 128], P(None, None, 'ha', 'wa'), may hold values from -6 to 6
- token_values: bfloat16 [16, 4, 64, 64, 128], P(None, None, 'ha', 'wa'), may hold values from -6 to 6
Outputs:
- attended: bfloat16 [16, 4, 64, 64, 128], P(None, None, 'ha', 'wa')
All inputs are finite; a program needn't handle non-finite values.
Results may differ from a plain program's by a relative error of at most 0.0055.
Values may be sent and summed in bfloat16 or wider, within the bound.
No kernel may reach another device: no remote copies, remote signals or barrier semaphores. Data moves between devices by JAX's collectives and lax.ppermute only.
A program may use at most 64 MiB of HBM per device.

v0:
```python
import functools

import jax
import jax.numpy as jnp
from jax import lax
from jax.experimental import pallas as pl
from jax.experimental.pallas import tpu as pltpu
from jax.sharding import Mesh, PartitionSpec as P

AXES = ("x", "yl", "core", "z", "yh")
SIZES = (4, 2, 2, 8, 2)
PLANE = ("x", "yl", "yh")
RING = 8
DH = 128
TOKENS = 64
LOG2E = 1.4426950408889634
FACTOR = DH ** (-0.5) * LOG2E
LIMIT = 2.0**100
TILE = 128
WIDTH = 1024
COST_SCALE = 10
VMEM = pl.BlockSpec(memory_space=pltpu.VMEM)
PARAMS = pltpu.CompilerParams(vmem_limit_bytes=28 << 20)


def dot(left, right, left_dim, right_dim):
    return lax.dot_general(
        left,
        right,
        (((left_dim,), (right_dim,)), ((), ())),
        preferred_element_type=jnp.float32,
    )


def fold_chunk(q, chunk_ref, state, exact):
    keys = chunk_ref[:, :TOKENS, :].reshape(-1, DH)
    values = chunk_ref[:, TOKENS:, :].reshape(-1, DH)
    scores = dot(keys, q, 1, 1)
    shift_row = None if state is None else state[0]
    shrink = None
    if exact:
        top = jnp.max(scores, axis=0, keepdims=True) * FACTOR
        if state is not None:
            top = jnp.maximum(shift_row, top)
            shrink = jnp.exp2(shift_row - top)
        shift_row = top
    weights = jnp.exp2(scores * FACTOR - shift_row)
    total = jnp.sum(weights, axis=0, keepdims=True)
    mixed = dot(values, weights.astype(jnp.bfloat16), 0, 0)
    if state is None:
        return (shift_row, total, mixed)
    if shrink is None:
        return (shift_row, state[1] + total, state[2] + mixed)
    return (shift_row, state[1] * shrink + total, state[2] * shrink + mixed)


def cost(queries, chunks):
    keys = sum(c.shape[0] * TOKENS for c in chunks)
    return pl.CostEstimate(
        flops=COST_SCALE * queries * keys * DH,
        bytes_accessed=4 * keys * DH,
        transcendentals=0,
    )


def each_tile(count, width, body):
    def step(i, carry):
        body(pl.multiple_of(i * width, width))
        return carry

    lax.fori_loop(0, count // width, step, 0)


def fold_kernel(n_chunks, first, q_ref, *refs):
    chunks = refs[:n_chunks]

    def tile(at):
        cols = pl.ds(at, WIDTH)
        state = None if first else tuple(r[:, cols] for r in refs[n_chunks : n_chunks + 3])
        for chunk in chunks:
            state = fold_chunk(q_ref[cols, :], chunk, state, state is None)
        for ref, value in zip(refs[-3:], state):
            ref[:, cols] = value

    each_tile(q_ref.shape[0], WIDTH, tile)


def fold(q, chunks, state):
    count = q.shape[0]
    first = state is None
    operands = (q, *chunks) + (() if first else tuple(state))
    base = 1 + len(chunks)
    row = jax.ShapeDtypeStruct((1, count), jnp.float32)
    return pl.pallas_call(
        functools.partial(fold_kernel, len(chunks), first),
        out_shape=(row, row, jax.ShapeDtypeStruct((DH, count), jnp.float32)),
        in_specs=[VMEM] * len(operands),
        out_specs=[VMEM] * 3,
        input_output_aliases={} if first else {base: 0, base + 1: 1, base + 2: 2},
        compiler_params=PARAMS,
        cost_estimate=cost(count, chunks),
        name="fold",
    )(*operands)


def last_kernel(n_new, n_all, away, q_ref, *refs):
    chunks = refs[:n_all]
    row_refs = refs[n_all : n_all + 3]
    acc_out, stats_out = refs[n_all + 3 :]
    half = q_ref.shape[0] // 2
    start = half if away else 0

    def finish(state, cols):
        top, total, acc = state
        acc_out[:, cols] = (acc / total).astype(jnp.bfloat16) if away else acc
        stats_out[0:1, cols] = top
        stats_out[1:2, cols] = total

    def tile(at):
        cols = pl.ds(start + at, WIDTH)
        state = tuple(r[:, cols] for r in row_refs)
        for chunk in chunks[:n_new]:
            state = fold_chunk(q_ref[cols, :], chunk, state, False)
        finish(state, pl.ds(at, WIDTH))

    each_tile(half, WIDTH, tile)

    @pl.when(jnp.logical_not(jnp.max(stats_out[1:2, :]) < LIMIT))
    def _():
        def again(at):
            q = q_ref[pl.ds(start + at, TILE), :]
            row = jnp.zeros((1, TILE), jnp.float32)
            state = (row - jnp.inf, row, jnp.zeros((DH, TILE), jnp.float32))
            for chunk in chunks:
                state = lax.fori_loop(
                    0,
                    chunk.shape[0],
                    lambda i, s, c=chunk: fold_chunk(q, c.at[pl.ds(i, 1)], s, True),
                    state,
                )
            finish(state, pl.ds(at, TILE))

        each_tile(half, TILE, again)


def last(q, new, old, state, away):
    half = q.shape[0] // 2
    operands = (q, *new, *old, *state)
    return pl.pallas_call(
        functools.partial(last_kernel, len(new), len(new) + len(old), away),
        out_shape=(
            jax.ShapeDtypeStruct((DH, half), jnp.bfloat16 if away else jnp.float32),
            jax.ShapeDtypeStruct((2, half), jnp.float32),
        ),
        in_specs=[VMEM] * len(operands),
        out_specs=[VMEM] * 2,
        compiler_params=PARAMS,
        cost_estimate=cost(half, new),
        name="last_away" if away else "last_own",
    )(*operands)


def join_kernel(own_ref, own_stats_ref, other_ref, other_stats_ref, out_ref):
    own_top, own_total = own_stats_ref[0:1, :], own_stats_ref[1:2, :]
    other_top, other_total = other_stats_ref[0:1, :], other_stats_ref[1:2, :]
    top = jnp.maximum(own_top, other_top)
    own_scale = jnp.exp2(own_top - top)
    other_scale = other_total * jnp.exp2(other_top - top)
    total = own_total * own_scale + other_scale
    joined = (
        own_ref[...] * own_scale + other_ref[...].astype(jnp.float32) * other_scale
    ) / total
    out_ref[...] = joined.T.astype(jnp.bfloat16)


def join(own, own_stats, other, other_stats):
    return pl.pallas_call(
        join_kernel,
        out_shape=jax.ShapeDtypeStruct(own.shape[::-1], jnp.bfloat16),
        in_specs=[VMEM] * 4,
        out_specs=VMEM,
        compiler_params=PARAMS,
        name="join",
    )(own, own_stats, other, other_stats)


def shift(block, axis, distance, size):
    return lax.ppermute(block, axis, [(i, (i + distance) % size) for i in range(size)])


def shards(token_queries, token_keys, token_values):
    shape = token_queries.shape
    heads = shape[0]
    flat = [a.reshape(heads, TOKENS, DH) for a in (token_queries, token_keys, token_values)]
    sent = jnp.concatenate(flat, axis=1)
    got = lax.all_to_all(sent, PLANE, split_axis=0, concat_axis=0, tiled=True)
    own_q = got[:, :TOKENS].reshape(heads * TOKENS, DH)
    chunk_a = got[: heads // 2, TOKENS:]
    chunk_b = got[heads // 2 :, TOKENS:]
    other_q = shift(own_q, "core", 1, 2)
    q = jnp.concatenate([own_q, other_q], axis=0)

    right_a, left_b = shift(chunk_a, "z", 1, RING), shift(chunk_b, "z", -1, RING)
    q, chunk_a, chunk_b = lax.optimization_barrier((q, chunk_a, chunk_b))
    right_b, left_a = shift(chunk_b, "z", 1, RING), shift(chunk_a, "z", -1, RING)
    state = fold(q, (chunk_a, chunk_b), None)
    seen = [chunk_a, chunk_b]
    for step in range(1, RING // 2):
        if step > 1:
            right_a, left_b = shift(right_a, "z", 1, RING), shift(left_b, "z", -1, RING)
            right_b, left_a = shift(right_b, "z", 1, RING), shift(left_a, "z", -1, RING)
        right_a, left_b, state = lax.optimization_barrier((right_a, left_b, state))
        state = fold(q, (right_a, left_b), state)
        right_b, left_a, state = lax.optimization_barrier((right_b, left_a, state))
        state = fold(q, (right_b, left_a), state)
        seen += [right_a, left_b, right_b, left_a]
    right_a, left_b = shift(right_a, "z", 1, RING), shift(left_b, "z", -1, RING)
    away, away_stats = last(q, (right_a, left_b), seen, state, True)
    other, other_stats = shift((away, away_stats), "core", 1, 2)
    own, own_stats = last(q, (right_a, left_b), seen, state, False)
    rows = join(own, own_stats, other, other_stats)
    back = lax.all_to_all(
        rows.reshape(shape), PLANE, split_axis=0, concat_axis=0, tiled=True
    )
    return back


def solution(mesh):
    fine = Mesh(mesh.devices.reshape(SIZES), AXES)
    placed = P(None, None, ("x", "yl", "core"), ("z", "yh"), None)
    return jax.shard_map(
        shards,
        mesh=fine,
        in_specs=(placed, placed, placed),
        out_specs=placed,
        check_vma=False,
    )
```

profile of v0, /device:TPU:1, one launch (start us, length us, event | category | flops | bytes accessed | tf_op | source)
XLA Modules:
  0.0 403.3 jit_solution(11478406231204047433)
XLA Ops:
  0.0 1.2 pad_maximum_fusion
  1.2 20.8 %all_to_all.10 = bf16[16,192,128]{2,1,0:T(8,128)(2,1)S(1)} all-to-all(bf16[16,192,128]{2,1,0:T(8,128)(2,1)S(1)} %pad_maximum_fusion), channel_id=1, replica_groups=mesh['x'=4,'yl'=2,'core'=2,'z'=8,'yh'=2] {'x','yl','yh'}, dimensions={0} | all-to-all | bytes 1572864 | tf_op jit(solution)/shard_map/all_to_all | solution.py:196
  22.0 2.1 collective-permute-start
  24.1 1.7 collective-permute-start.1
  25.8 4.0 collective-permute-start.2
  30.0 2.7 collective-permute-start.6
  32.7 3.2 fold.7
  36.4 2.7 collective-permute-start.4
  39.1 2.4 fold.8
  42.1 2.6 collective-permute-start.10
  44.6 2.4 fold.9
  47.7 2.7 collective-permute-start.8
  50.4 2.4 fold.10
  52.9 3.0 collective-permute-start.14
  55.9 2.4 fold.11
  58.4 3.1 collective-permute-start.12
  61.5 2.4 fold.12
  63.9 2.4 fold.13
  66.3 2.7 collective-permute-done.11.refs_0_
  69.0 1.2 last_away.1
  70.2 2.5 collective-permute-start.15
  72.8 1.2 last_own.1
  74.2 328.4 %all_to_all.11 = bf16[16,4,4,4,128]{4,3,2,1,0:T(4,128)(2,1)S(1)} all-to-all(bf16[16,4,4,4,128]{4,3,2,1,0:T(4,128)(2,1)S(1)} %bitcast.5), channel_id=1, replica_groups=mesh['x'=4,'yl'=2,'core'=2,'z'=8,'yh'=2] {'x','yl','yh'}, dimensions={0} | all-to-all | bytes 524288 | tf_op jit(solution)/shard_map/all_to_all | solution.py:222
  402.6 0.7 copy.41
  (27 shorter events, 2.4 us)
Async XLA Ops:
  22.0 7.9 %collective-permute-start = (bf16[1024,128]{1,0:T(8,128)(2,1)S(1)}, bf16[1024,128]{1,0:T(8,128)(2,1)S(1)}, u32[]{:S(2)}, u32[]{:S(2)}) collective-permute-start(bf16[1024,128]{1,0:T(8,128)(2,1)S(1)} %bitcast.6), channel_id=1, source_target_pairs={{0,16},{16,0},{1,17},{17,1},{2,18},{18,2},{3,19},{19,3},{4,20},{20... | collective-permute-start | bytes 786440 | tf_op jit(solution)/shard_map/ppermute | solution.py:188
  24.1 12.3 %collective-permute-start.1 = (bf16[8,128,128]{2,1,0:T(8,128)(2,1)S(1)}, bf16[8,128,128]{2,1,0:T(8,128)(2,1)S(1)}, u32[]{:S(2)}, u32[]{:S(2)}) collective-permute-start(bf16[8,128,128]{2,1,0:T(8,128)(2,1)S(1)} %get-tuple-element.64.refs_0_.refs_2_), channel_id=1, source_target_pairs={{0,2},{2,4},{4,6},{6,8},{8,10},{10,12},{12,14},{14,0},{1,3},{3,5},... | collective-permute-start | bytes 786440 | tf_op jit(solution)/shard_map/ppermute | solution.py:188
  25.8 10.6 %collective-permute-start.2 = (bf16[8,128,128]{2,1,0:T(8,128)(2,1)S(1)}, bf16[8,128,128]{2,1,0:T(8,128)(2,1)S(1)}, u32[]{:S(2)}, u32[]{:S(2)}) collective-permute-start(bf16[8,128,128]{2,1,0:T(8,128)(2,1)S(1)} %get-tuple-element.65.refs_1_.refs_3_), channel_id=1, source_target_pairs={{0,14},{2,0},{4,2},{6,4},{8,6},{10,8},{12,10},{14,12},{1,15},{3,1}... | collective-permute-start | bytes 786440 | tf_op jit(solution)/shard_map/ppermute | solution.py:188
  29.9 12.1 %collective-permute-start.5 = (bf16[8,128,128]{2,1,0:T(8,128)(2,1)S(1)}, bf16[8,128,128]{2,1,0:T(8,128)(2,1)S(1)}, u32[]{:S(2)}, u32[]{:S(2)}) collective-permute-start(bf16[8,128,128]{2,1,0:T(8,128)(2,1)S(1)} %get-tuple-element.65.refs_1_.refs_3_), channel_id=1, source_target_pairs={{0,2},{2,4},{4,6},{6,8},{8,10},{10,12},{12,14},{14,0},{1,3},{3,5},... | collective-permute-start | bytes 786440 | tf_op jit(solution)/shard_map/ppermute | solution.py:188
  30.0 12.1 %collective-permute-start.6 = (bf16[8,128,128]{2,1,0:T(8,128)(2,1)S(1)}, bf16[8,128,128]{2,1,0:T(8,128)(2,1)S(1)}, u32[]{:S(2)}, u32[]{:S(2)}) collective-permute-start(bf16[8,128,128]{2,1,0:T(8,128)(2,1)S(1)} %get-tuple-element.64.refs_0_.refs_2_), channel_id=1, source_target_pairs={{0,14},{2,0},{4,2},{6,4},{8,6},{10,8},{12,10},{14,12},{1,15},{3,1}... | collective-permute-start | bytes 786440 | tf_op jit(solution)/shard_map/ppermute | solution.py:188
  36.4 11.2 %collective-permute-start.3 = (bf16[8,128,128]{2,1,0:T(8,128)(2,1)S(1)}, bf16[8,128,128]{2,1,0:T(8,128)(2,1)S(1)}, u32[]{:S(2)}, u32[]{:S(2)}) collective-permute-start(bf16[8,128,128]{2,1,0:T(8,128)(2,1)S(1)} %collective-permute-done.1.refs_0_.refs_4_), channel_id=1, source_target_pairs={{0,2},{2,4},{4,6},{6,8},{8,10},{10,12},{12,14},{14,0},{1,3},{3,5},... | collective-permute-start | bytes 786440 | tf_op jit(solution)/shard_map/ppermute | solution.py:188
  36.4 11.2 %collective-permute-start.4 = (bf16[8,128,128]{2,1,0:T(8,128)(2,1)S(1)}, bf16[8,128,128]{2,1,0:T(8,128)(2,1)S(1)}, u32[]{:S(2)}, u32[]{:S(2)}) collective-permute-start(bf16[8,128,128]{2,1,0:T(8,128)(2,1)S(1)} %collective-permute-done.2.refs_1_.refs_5_), channel_id=1, source_target_pairs={{0,14},{2,0},{4,2},{6,4},{8,6},{10,8},{12,10},{14,12},{1,15},{3,1}... | collective-permute-start | bytes 786440 | tf_op jit(solution)/shard_map/ppermute | solution.py:188
  42.1 10.7 %collective-permute-start.10 = (bf16[8,128,128]{2,1,0:T(8,128)(2,1)S(1)}, bf16[8,128,128]{2,1,0:T(8,128)(2,1)S(1)}, u32[]{:S(2)}, u32[]{:S(2)}) collective-permute-start(bf16[8,128,128]{2,1,0:T(8,128)(2,1)S(1)} %collective-permute-done.6.refs_1_.refs_7_), channel_id=1, source_target_pairs={{0,14},{2,0},{4,2},{6,4},{8,6},{10,8},{12,10},{14,12},{1,15},{3,1}... | collective-permute-start | bytes 786440 | tf_op jit(solution)/shard_map/ppermute | solution.py:188
  44.6 8.2 %collective-permute-start.9 = (bf16[8,128,128]{2,1,0:T(8,128)(2,1)S(1)}, bf16[8,128,128]{2,1,0:T(8,128)(2,1)S(1)}, u32[]{:S(2)}, u32[]{:S(2)}) collective-permute-start(bf16[8,128,128]{2,1,0:T(8,128)(2,1)S(1)} %collective-permute-done.5.refs_0_.refs_6_), channel_id=1, source_target_pairs={{0,2},{2,4},{4,6},{6,8},{8,10},{10,12},{12,14},{14,0},{1,3},{3,5},... | collective-permute-start | bytes 786440 | tf_op jit(solution)/shard_map/ppermute | solution.py:188
  47.7 10.6 %collective-permute-start.7 = (bf16[8,128,128]{2,1,0:T(8,128)(2,1)S(1)}, bf16[8,128,128]{2,1,0:T(8,128)(2,1)S(1)}, u32[]{:S(2)}, u32[]{:S(2)}) collective-permute-start(bf16[8,128,128]{2,1,0:T(8,128)(2,1)S(1)} %collective-permute-done.3.refs_0_.refs_8_), channel_id=1, source_target_pairs={{0,2},{2,4},{4,6},{6,8},{8,10},{10,12},{12,14},{14,0},{1,3},{3,5},... | collective-permute-start | bytes 786440 | tf_op jit(solution)/shard_map/ppermute | solution.py:188
  47.7 10.6 %collective-permute-start.8 = (bf16[8,128,128]{2,1,0:T(8,128)(2,1)S(1)}, bf16[8,128,128]{2,1,0:T(8,128)(2,1)S(1)}, u32[]{:S(2)}, u32[]{:S(2)}) collective-permute-start(bf16[8,128,128]{2,1,0:T(8,128)(2,1)S(1)} %collective-permute-done.4.refs_1_.refs_9_), channel_id=1, source_target_pairs={{0,14},{2,0},{4,2},{6,4},{8,6},{10,8},{12,10},{14,12},{1,15},{3,1}... | collective-permute-start | bytes 786440 | tf_op jit(solution)/shard_map/ppermute | solution.py:188
  52.8 11.1 %collective-permute-start.13 = (bf16[8,128,128]{2,1,0:T(8,128)(2,1)S(1)}, bf16[8,128,128]{2,1,0:T(8,128)(2,1)S(1)}, u32[]{:S(2)}, u32[]{:S(2)}) collective-permute-start(bf16[8,128,128]{2,1,0:T(8,128)(2,1)S(1)} %collective-permute-done.9.refs_0_.refs_10_), channel_id=1, source_target_pairs={{0,2},{2,4},{4,6},{6,8},{8,10},{10,12},{12,14},{14,0},{1,3},{3,5},... | collective-permute-start | bytes 786440 | tf_op jit(solution)/shard_map/ppermute | solution.py:188
  52.9 11.0 %collective-permute-start.14 = (bf16[8,128,128]{2,1,0:T(8,128)(2,1)S(1)}, bf16[8,128,128]{2,1,0:T(8,128)(2,1)S(1)}, u32[]{:S(2)}, u32[]{:S(2)}) collective-permute-start(bf16[8,128,128]{2,1,0:T(8,128)(2,1)S(1)} %collective-permute-done.10.refs_1_.refs_11_), channel_id=1, source_target_pairs={{0,14},{2,0},{4,2},{6,4},{8,6},{10,8},{12,10},{14,12},{1,15},{3,1}... | collective-permute-start | bytes 786440 | tf_op jit(solution)/shard_map/ppermute | solution.py:188
  58.3 10.7 %collective-permute-start.11 = (bf16[8,128,128]{2,1,0:T(8,128)(2,1)S(1)}, bf16[8,128,128]{2,1,0:T(8,128)(2,1)S(1)}, u32[]{:S(2)}, u32[]{:S(2)}) collective-permute-start(bf16[8,128,128]{2,1,0:T(8,128)(2,1)S(1)} %collective-permute-done.7.refs_0_.refs_12_), channel_id=1, source_target_pairs={{0,2},{2,4},{4,6},{6,8},{8,10},{10,12},{12,14},{14,0},{1,3},{3,5},... | collective-permute-start | bytes 786440 | tf_op jit(solution)/shard_map/ppermute | solution.py:188
  58.4 10.6 %collective-permute-start.12 = (bf16[8,128,128]{2,1,0:T(8,128)(2,1)S(1)}, bf16[8,128,128]{2,1,0:T(8,128)(2,1)S(1)}, u32[]{:S(2)}, u32[]{:S(2)}) collective-permute-start(bf16[8,128,128]{2,1,0:T(8,128)(2,1)S(1)} %collective-permute-done.8.refs_1_.refs_13_), channel_id=1, source_target_pairs={{0,14},{2,0},{4,2},{6,4},{8,6},{10,8},{12,10},{14,12},{1,15},{3,1}... | collective-permute-start | bytes 786440 | tf_op jit(solution)/shard_map/ppermute | solution.py:188
  70.2 3.8 collective-permute-start.15
  72.7 1.3 collective-permute-start.16
where the time goes:
time: 403 us
  blocking collectives  349 us (87%)
  starting transfers between devices  27.3 us (7%)
  Pallas kernels  20.2 us (5%)
  waiting for transfers between devices  4.47 us (1%)
    all_to_all x1, blocking collectives, shards(): lax.all_to_all(rows.reshape(shape), PLANE, split_axis=0, concat_axis=0, t...  328 us
    ppermute x17, starting transfers between devices, shift(): lax.ppermute(block, axis, [(i, (i + distance) % size) for i in range(size)])  27.3 us
    all_to_all x1, blocking collectives, shards(): got = lax.all_to_all(sent, PLANE, split_axis=0, concat_axis=0, tiled=True)  20.8 us
    pallas_call x7, Pallas kernels, fold(): pl.pallas_call(functools.partial(fold_kernel, len(chunks), first), out_sh...  17.6 us
  transfers between devices with their start and end apart: 17, of which 4 were waited for; matrix products, arithmetic and copies ran while one was open for 0% of the time, Pallas kernels for 5%

commit v1 on v0

--- a/solution.py
+++ b/solution.py
@@ -9,7 +9,7 @@
 
 AXES = ("x", "yl", "core", "z", "yh")
 SIZES = (4, 2, 2, 8, 2)
-PLANE = ("x", "yl", "yh")
+PLANE = ("yh", "x", "yl")
 RING = 8
 DH = 128
 TOKENS = 64

time: 403 us -> 403 us (level)
  no operation moved by 1% of the time
where the time goes in v1:
time: 403 us; the launch traced here: 402 us
  blocking collectives  348 us (86%)
  starting transfers between devices  27 us (7%)
  Pallas kernels  20.2 us (5%)
  waiting for transfers between devices  4.47 us (1%)
    all_to_all x1, blocking collectives, shards(): lax.all_to_all(rows.reshape(shape), PLANE, split_axis=0, concat_axis=0, t...  328 us
    ppermute x17, starting transfers between devices, shift(): lax.ppermute(block, axis, [(i, (i + distance) % size) for i in range(size)])  27 us
    all_to_all x1, blocking collectives, shards(): got = lax.all_to_all(sent, PLANE, split_axis=0, concat_axis=0, tiled=True)  20.8 us
    pallas_call x7, Pallas kernels, fold(): pl.pallas_call(functools.partial(fold_kernel, len(chunks), first), out_sh...  17.6 us
  transfers between devices with their start and end apart: 17, of which 4 were waited for; matrix products, arithmetic and copies ran while one was open for 0% of the time, Pallas kernels for 5%

profile of v1, /device:TPU:1, one launch (start us, length us, event | category | flops | bytes accessed | tf_op | source)
XLA Modules:
  0.0 402.3 jit_solution(3455169639400788441)
XLA Ops:
  0.0 1.2 pad_maximum_fusion
  1.2 20.8 %all_to_all.10 = bf16[16,192,128]{2,1,0:T(8,128)(2,1)S(1)} all-to-all(bf16[16,192,128]{2,1,0:T(8,128)(2,1)S(1)} %pad_maximum_fusion), channel_id=1, replica_groups=mesh['x'=4,'yl'=2,'core'=2,'z'=8,'yh'=2] {'yh','x','yl'}, dimensions={0} | all-to-all | bytes 1572864 | tf_op jit(solution)/shard_map/all_to_all | solution.py:196
  22.0 1.8 collective-permute-start
  23.8 1.7 collective-permute-start.1
  25.5 4.0 %collective-permute-start.2 = (bf16[8,128,128]{2,1,0:T(8,128)(2,1)S(1)}, bf16[8,128,128]{2,1,0:T(8,128)(2,1)S(1)}, u32[]{:S(2)}, u32[]{:S(2)}) collective-permute-start(bf16[8,128,128]{2,1,0:T(8,128)(2,1)S(1)} %get-tuple-element.65.refs_1_.refs_3_), channel_id=1, source_target_pairs={{0,14},{2,0},{4,2},{6,4},{8,6},{10,8},{12,10},{14,12},{1,15},{3,1}... | collective-permute-start | bytes 786440 | tf_op jit(solution)/shard_map/ppermute | solution.py:188
  29.7 2.7 collective-permute-start.6
  32.3 3.2 fold.7
  36.1 2.7 collective-permute-start.4
  38.8 2.4 fold.8
  41.7 2.6 collective-permute-start.10
  44.3 2.4 fold.9
  47.3 2.7 collective-permute-start.8
  50.0 2.4 fold.10
  52.5 3.0 collective-permute-start.14
  55.5 2.4 fold.11
  58.0 3.1 collective-permute-start.12
  61.1 2.4 fold.12
  63.5 2.4 fold.13
  66.0 2.7 collective-permute-done.11.refs_0_
  68.7 1.2 last_away.1
  69.9 2.5 collective-permute-start.15
  72.5 1.2 last_own.1
  73.9 327.7 %all_to_all.11 = bf16[16,4,4,4,128]{4,3,2,1,0:T(4,128)(2,1)S(1)} all-to-all(bf16[16,4,4,4,128]{4,3,2,1,0:T(4,128)(2,1)S(1)} %bitcast.5), channel_id=1, replica_groups=mesh['x'=4,'yl'=2,'core'=2,'z'=8,'yh'=2] {'yh','x','yl'}, dimensions={0} | all-to-all | bytes 524288 | tf_op jit(solution)/shard_map/all_to_all | solution.py:222
  401.6 0.7 copy.41
  (27 shorter events, 2.4 us)
Async XLA Ops:
  22.0 7.5 %collective-permute-start = (bf16[1024,128]{1,0:T(8,128)(2,1)S(1)}, bf16[1024,128]{1,0:T(8,128)(2,1)S(1)}, u32[]{:S(2)}, u32[]{:S(2)}) collective-permute-start(bf16[1024,128]{1,0:T(8,128)(2,1)S(1)} %bitcast.6), channel_id=1, source_target_pairs={{0,16},{16,0},{1,17},{17,1},{2,18},{18,2},{3,19},{19,3},{4,20},{20... | collective-permute-start | bytes 786440 | tf_op jit(solution)/shard_map/ppermute | solution.py:188
  23.8 12.3 %collective-permute-start.1 = (bf16[8,128,128]{2,1,0:T(8,128)(2,1)S(1)}, bf16[8,128,128]{2,1,0:T(8,128)(2,1)S(1)}, u32[]{:S(2)}, u32[]{:S(2)}) collective-permute-start(bf16[8,128,128]{2,1,0:T(8,128)(2,1)S(1)} %get-tuple-element.64.refs_0_.refs_2_), channel_id=1, source_target_pairs={{0,2},{2,4},{4,6},{6,8},{8,10},{10,12},{12,14},{14,0},{1,3},{3,5},... | collective-permute-start | bytes 786440 | tf_op jit(solution)/shard_map/ppermute | solution.py:188
  25.5 10.6 %collective-permute-start.2 = (bf16[8,128,128]{2,1,0:T(8,128)(2,1)S(1)}, bf16[8,128,128]{2,1,0:T(8,128)(2,1)S(1)}, u32[]{:S(2)}, u32[]{:S(2)}) collective-permute-start(bf16[8,128,128]{2,1,0:T(8,128)(2,1)S(1)} %get-tuple-element.65.refs_1_.refs_3_), channel_id=1, source_target_pairs={{0,14},{2,0},{4,2},{6,4},{8,6},{10,8},{12,10},{14,12},{1,15},{3,1}... | collective-permute-start | bytes 786440 | tf_op jit(solution)/shard_map/ppermute | solution.py:188
  29.6 12.1 %collective-permute-start.5 = (bf16[8,128,128]{2,1,0:T(8,128)(2,1)S(1)}, bf16[8,128,128]{2,1,0:T(8,128)(2,1)S(1)}, u32[]{:S(2)}, u32[]{:S(2)}) collective-permute-start(bf16[8,128,128]{2,1,0:T(8,128)(2,1)S(1)} %get-tuple-element.65.refs_1_.refs_3_), channel_id=1, source_target_pairs={{0,2},{2,4},{4,6},{6,8},{8,10},{10,12},{12,14},{14,0},{1,3},{3,5},... | collective-permute-start | bytes 786440 | tf_op jit(solution)/shard_map/ppermute | solution.py:188
  29.7 12.1 %collective-permute-start.6 = (bf16[8,128,128]{2,1,0:T(8,128)(2,1)S(1)}, bf16[8,128,128]{2,1,0:T(8,128)(2,1)S(1)}, u32[]{:S(2)}, u32[]{:S(2)}) collective-permute-start(bf16[8,128,128]{2,1,0:T(8,128)(2,1)S(1)} %get-tuple-element.64.refs_0_.refs_2_), channel_id=1, source_target_pairs={{0,14},{2,0},{4,2},{6,4},{8,6},{10,8},{12,10},{14,12},{1,15},{3,1}... | collective-permute-start | bytes 786440 | tf_op jit(solution)/shard_map/ppermute | solution.py:188
  36.1 11.2 %collective-permute-start.3 = (bf16[8,128,128]{2,1,0:T(8,128)(2,1)S(1)}, bf16[8,128,128]{2,1,0:T(8,128)(2,1)S(1)}, u32[]{:S(2)}, u32[]{:S(2)}) collective-permute-start(bf16[8,128,128]{2,1,0:T(8,128)(2,1)S(1)} %collective-permute-done.1.refs_0_.refs_4_), channel_id=1, source_target_pairs={{0,2},{2,4},{4,6},{6,8},{8,10},{10,12},{12,14},{14,0},{1,3},{3,5},... | collective-permute-start | bytes 786440 | tf_op jit(solution)/shard_map/ppermute | solution.py:188
  36.1 11.2 %collective-permute-start.4 = (bf16[8,128,128]{2,1,0:T(8,128)(2,1)S(1)}, bf16[8,128,128]{2,1,0:T(8,128)(2,1)S(1)}, u32[]{:S(2)}, u32[]{:S(2)}) collective-permute-start(bf16[8,128,128]{2,1,0:T(8,128)(2,1)S(1)} %collective-permute-done.2.refs_1_.refs_5_), channel_id=1, source_target_pairs={{0,14},{2,0},{4,2},{6,4},{8,6},{10,8},{12,10},{14,12},{1,15},{3,1}... | collective-permute-start | bytes 786440 | tf_op jit(solution)/shard_map/ppermute | solution.py:188
  41.7 10.7 %collective-permute-start.10 = (bf16[8,128,128]{2,1,0:T(8,128)(2,1)S(1)}, bf16[8,128,128]{2,1,0:T(8,128)(2,1)S(1)}, u32[]{:S(2)}, u32[]{:S(2)}) collective-permute-start(bf16[8,128,128]{2,1,0:T(8,128)(2,1)S(1)} %collective-permute-done.6.refs_1_.refs_7_), channel_id=1, source_target_pairs={{0,14},{2,0},{4,2},{6,4},{8,6},{10,8},{12,10},{14,12},{1,15},{3,1}... | collective-permute-start | bytes 786440 | tf_op jit(solution)/shard_map/ppermute | solution.py:188
  44.3 8.2 %collective-permute-start.9 = (bf16[8,128,128]{2,1,0:T(8,128)(2,1)S(1)}, bf16[8,128,128]{2,1,0:T(8,128)(2,1)S(1)}, u32[]{:S(2)}, u32[]{:S(2)}) collective-permute-start(bf16[8,128,128]{2,1,0:T(8,128)(2,1)S(1)} %collective-permute-done.5.refs_0_.refs_6_), channel_id=1, source_target_pairs={{0,2},{2,4},{4,6},{6,8},{8,10},{10,12},{12,14},{14,0},{1,3},{3,5},... | collective-permute-start | bytes 786440 | tf_op jit(solution)/shard_map/ppermute | solution.py:188
  47.3 10.6 %collective-permute-start.7 = (bf16[8,128,128]{2,1,0:T(8,128)(2,1)S(1)}, bf16[8,128,128]{2,1,0:T(8,128)(2,1)S(1)}, u32[]{:S(2)}, u32[]{:S(2)}) collective-permute-start(bf16[8,128,128]{2,1,0:T(8,128)(2,1)S(1)} %collective-permute-done.3.refs_0_.refs_8_), channel_id=1, source_target_pairs={{0,2},{2,4},{4,6},{6,8},{8,10},{10,12},{12,14},{14,0},{1,3},{3,5},... | collective-permute-start | bytes 786440 | tf_op jit(solution)/shard_map/ppermute | solution.py:188
  47.3 10.6 %collective-permute-start.8 = (bf16[8,128,128]{2,1,0:T(8,128)(2,1)S(1)}, bf16[8,128,128]{2,1,0:T(8,128)(2,1)S(1)}, u32[]{:S(2)}, u32[]{:S(2)}) collective-permute-start(bf16[8,128,128]{2,1,0:T(8,128)(2,1)S(1)} %collective-permute-done.4.refs_1_.refs_9_), channel_id=1, source_target_pairs={{0,14},{2,0},{4,2},{6,4},{8,6},{10,8},{12,10},{14,12},{1,15},{3,1}... | collective-permute-start | bytes 786440 | tf_op jit(solution)/shard_map/ppermute | solution.py:188
  52.4 11.1 %collective-permute-start.13 = (bf16[8,128,128]{2,1,0:T(8,128)(2,1)S(1)}, bf16[8,128,128]{2,1,0:T(8,128)(2,1)S(1)}, u32[]{:S(2)}, u32[]{:S(2)}) collective-permute-start(bf16[8,128,128]{2,1,0:T(8,128)(2,1)S(1)} %collective-permute-done.9.refs_0_.refs_10_), channel_id=1, source_target_pairs={{0,2},{2,4},{4,6},{6,8},{8,10},{10,12},{12,14},{14,0},{1,3},{3,5},... | collective-permute-start | bytes 786440 | tf_op jit(solution)/shard_map/ppermute | solution.py:188
  52.5 11.0 %collective-permute-start.14 = (bf16[8,128,128]{2,1,0:T(8,128)(2,1)S(1)}, bf16[8,128,128]{2,1,0:T(8,128)(2,1)S(1)}, u32[]{:S(2)}, u32[]{:S(2)}) collective-permute-start(bf16[8,128,128]{2,1,0:T(8,128)(2,1)S(1)} %collective-permute-done.10.refs_1_.refs_11_), channel_id=1, source_target_pairs={{0,14},{2,0},{4,2},{6,4},{8,6},{10,8},{12,10},{14,12},{1,15},{3,1}... | collective-permute-start | bytes 786440 | tf_op jit(solution)/shard_map/ppermute | solution.py:188
  57.9 10.7 %collective-permute-start.11 = (bf16[8,128,128]{2,1,0:T(8,128)(2,1)S(1)}, bf16[8,128,128]{2,1,0:T(8,128)(2,1)S(1)}, u32[]{:S(2)}, u32[]{:S(2)}) collective-permute-start(bf16[8,128,128]{2,1,0:T(8,128)(2,1)S(1)} %collective-permute-done.7.refs_0_.refs_12_), channel_id=1, source_target_pairs={{0,2},{2,4},{4,6},{6,8},{8,10},{10,12},{12,14},{14,0},{1,3},{3,5},... | collective-permute-start | bytes 786440 | tf_op jit(solution)/shard_map/ppermute | solution.py:188
  58.0 10.6 %collective-permute-start.12 = (bf16[8,128,128]{2,1,0:T(8,128)(2,1)S(1)}, bf16[8,128,128]{2,1,0:T(8,128)(2,1)S(1)}, u32[]{:S(2)}, u32[]{:S(2)}) collective-permute-start(bf16[8,128,128]{2,1,0:T(8,128)(2,1)S(1)} %collective-permute-done.8.refs_1_.refs_13_), channel_id=1, source_target_pairs={{0,14},{2,0},{4,2},{6,4},{8,6},{10,8},{12,10},{14,12},{1,15},{3,1}... | collective-permute-start | bytes 786440 | tf_op jit(solution)/shard_map/ppermute | solution.py:188
  69.9 3.8 collective-permute-start.15
  72.4 1.3 collective-permute-start.16

commit v2 on v1

--- a/solution.py
+++ b/solution.py
@@ -17,7 +17,7 @@
 FACTOR = DH ** (-0.5) * LOG2E
 LIMIT = 2.0**100
 TILE = 128
-WIDTH = 1024
+WIDTH = 2048
 COST_SCALE = 10
 VMEM = pl.BlockSpec(memory_space=pltpu.VMEM)
 PARAMS = pltpu.CompilerParams(vmem_limit_bytes=28 << 20)
@@ -117,13 +117,13 @@
         stats_out[1:2, cols] = total
 
     def tile(at):
-        cols = pl.ds(start + at, WIDTH)
+        cols = pl.ds(start + at, min(WIDTH, half))
         state = tuple(r[:, cols] for r in row_refs)
         for chunk in chunks[:n_new]:
             state = fold_chunk(q_ref[cols, :], chunk, state, False)
-        finish(state, pl.ds(at, WIDTH))
-
-    each_tile(half, WIDTH, tile)
+        finish(state, pl.ds(at, min(WIDTH, half)))
+
+    each_tile(half, min(WIDTH, half), tile)
 
     @pl.when(jnp.logical_not(jnp.max(stats_out[1:2, :]) < LIMIT))
     def _():

time: 403 us -> 402 us (level)
  transfers between devices with their start and end apart: 17 -> 17, of which waited for: 4 -> 4; matrix products, arithmetic and copies ran while one was open for 0% -> 0% of each run, Pallas kernels for 5% -> 4%
where the time goes in v2:
time: 402 us; the launch traced here: 401 us
  blocking collectives  347 us (86%)
  starting transfers between devices  27.4 us (7%)
  Pallas kernels  18.7 us (5%)
  waiting for transfers between devices  5.53 us (1%)
    all_to_all x1, blocking collectives, shards(): lax.all_to_all(rows.reshape(shape), PLANE, split_axis=0, concat_axis=0, t...  326 us
    ppermute x17, starting transfers between devices, shift(): lax.ppermute(block, axis, [(i, (i + distance) % size) for i in range(size)])  27.4 us
    all_to_all x1, blocking collectives, shards(): got = lax.all_to_all(sent, PLANE, split_axis=0, concat_axis=0, tiled=True)  20.8 us
    pallas_call x7, Pallas kernels, fold(): pl.pallas_call(functools.partial(fold_kernel, len(chunks), first), out_sh...  16.1 us
  transfers between devices with their start and end apart: 17, of which 4 were waited for; matrix products, arithmetic and copies ran while one was open for 0% of the time, Pallas kernels for 4%

profile of v2, /device:TPU:1, one launch (start us, length us, event | category | flops | bytes accessed | tf_op | source)
XLA Modules:
  0.0 400.8 jit_solution(18042789295545178164)
XLA Ops:
  0.0 1.2 pad_maximum_fusion
  1.2 20.8 %all_to_all.10 = bf16[16,192,128]{2,1,0:T(8,128)(2,1)S(1)} all-to-all(bf16[16,192,128]{2,1,0:T(8,128)(2,1)S(1)} %pad_maximum_fusion), channel_id=1, replica_groups=mesh['x'=4,'yl'=2,'core'=2,'z'=8,'yh'=2] {'yh','x','yl'}, dimensions={0} | all-to-all | bytes 1572864 | tf_op jit(solution)/shard_map/all_to_all | solution.py:196
  22.0 1.8 collective-permute-start
  23.8 1.7 collective-permute-start.1
  25.5 4.0 %collective-permute-start.2 = (bf16[8,128,128]{2,1,0:T(8,128)(2,1)S(1)}, bf16[8,128,128]{2,1,0:T(8,128)(2,1)S(1)}, u32[]{:S(2)}, u32[]{:S(2)}) collective-permute-start(bf16[8,128,128]{2,1,0:T(8,128)(2,1)S(1)} %get-tuple-element.65.refs_1_.refs_3_), channel_id=1, source_target_pairs={{0,14},{2,0},{4,2},{6,4},{8,6},{10,8},{12,10},{14,12},{1,15},{3,1}... | collective-permute-start | bytes 786440 | tf_op jit(solution)/shard_map/ppermute | solution.py:188
  29.7 2.7 collective-permute-start.6
  32.3 2.9 fold.7
  35.2 0.9 collective-permute-done.1.refs_0_.refs_4_
  36.1 2.7 collective-permute-start.4
  38.8 2.2 fold.8
  41.7 2.6 collective-permute-start.10
  44.3 2.2 fold.9
  47.3 2.7 collective-permute-start.8
  50.0 2.2 fold.10
  52.3 3.2 collective-permute-start.14
  55.5 2.2 fold.11
  57.8 3.3 collective-permute-start.12
  61.1 2.2 fold.12
  63.4 2.2 fold.13
  65.6 3.1 collective-permute-done.11.refs_0_
  68.7 1.2 last_away.1
  69.9 2.5 collective-permute-start.15
  72.5 1.2 last_own.1
  73.9 326.2 %all_to_all.11 = bf16[16,4,4,4,128]{4,3,2,1,0:T(4,128)(2,1)S(1)} all-to-all(bf16[16,4,4,4,128]{4,3,2,1,0:T(4,128)(2,1)S(1)} %bitcast.5), channel_id=1, replica_groups=mesh['x'=4,'yl'=2,'core'=2,'z'=8,'yh'=2] {'yh','x','yl'}, dimensions={0} | all-to-all | bytes 524288 | tf_op jit(solution)/shard_map/all_to_all | solution.py:222
  (27 shorter events, 2.9 us)
Async XLA Ops:
  22.0 7.5 %collective-permute-start = (bf16[1024,128]{1,0:T(8,128)(2,1)S(1)}, bf16[1024,128]{1,0:T(8,128)(2,1)S(1)}, u32[]{:S(2)}, u32[]{:S(2)}) collective-permute-start(bf16[1024,128]{1,0:T(8,128)(2,1)S(1)} %bitcast.6), channel_id=1, source_target_pairs={{0,16},{16,0},{1,17},{17,1},{2,18},{18,2},{3,19},{19,3},{4,20},{20... | collective-permute-start | bytes 786440 | tf_op jit(solution)/shard_map/ppermute | solution.py:188
  23.8 12.3 %collective-permute-start.1 = (bf16[8,128,128]{2,1,0:T(8,128)(2,1)S(1)}, bf16[8,128,128]{2,1,0:T(8,128)(2,1)S(1)}, u32[]{:S(2)}, u32[]{:S(2)}) collective-permute-start(bf16[8,128,128]{2,1,0:T(8,128)(2,1)S(1)} %get-tuple-element.64.refs_0_.refs_2_), channel_id=1, source_target_pairs={{0,2},{2,4},{4,6},{6,8},{8,10},{10,12},{12,14},{14,0},{1,3},{3,5},... | collective-permute-start | bytes 786440 | tf_op jit(solution)/shard_map/ppermute | solution.py:188
  25.5 10.6 %collective-permute-start.2 = (bf16[8,128,128]{2,1,0:T(8,128)(2,1)S(1)}, bf16[8,128,128]{2,1,0:T(8,128)(2,1)S(1)}, u32[]{:S(2)}, u32[]{:S(2)}) collective-permute-start(bf16[8,128,128]{2,1,0:T(8,128)(2,1)S(1)} %get-tuple-element.65.refs_1_.refs_3_), channel_id=1, source_target_pairs={{0,14},{2,0},{4,2},{6,4},{8,6},{10,8},{12,10},{14,12},{1,15},{3,1}... | collective-permute-start | bytes 786440 | tf_op jit(solution)/shard_map/ppermute | solution.py:188
  29.6 12.1 %collective-permute-start.5 = (bf16[8,128,128]{2,1,0:T(8,128)(2,1)S(1)}, bf16[8,128,128]{2,1,0:T(8,128)(2,1)S(1)}, u32[]{:S(2)}, u32[]{:S(2)}) collective-permute-start(bf16[8,128,128]{2,1,0:T(8,128)(2,1)S(1)} %get-tuple-element.65.refs_1_.refs_3_), channel_id=1, source_target_pairs={{0,2},{2,4},{4,6},{6,8},{8,10},{10,12},{12,14},{14,0},{1,3},{3,5},... | collective-permute-start | bytes 786440 | tf_op jit(solution)/shard_map/ppermute | solution.py:188
  29.7 12.1 %collective-permute-start.6 = (bf16[8,128,128]{2,1,0:T(8,128)(2,1)S(1)}, bf16[8,128,128]{2,1,0:T(8,128)(2,1)S(1)}, u32[]{:S(2)}, u32[]{:S(2)}) collective-permute-start(bf16[8,128,128]{2,1,0:T(8,128)(2,1)S(1)} %get-tuple-element.64.refs_0_.refs_2_), channel_id=1, source_target_pairs={{0,14},{2,0},{4,2},{6,4},{8,6},{10,8},{12,10},{14,12},{1,15},{3,1}... | collective-permute-start | bytes 786440 | tf_op jit(solution)/shard_map/ppermute | solution.py:188
  36.1 11.2 %collective-permute-start.3 = (bf16[8,128,128]{2,1,0:T(8,128)(2,1)S(1)}, bf16[8,128,128]{2,1,0:T(8,128)(2,1)S(1)}, u32[]{:S(2)}, u32[]{:S(2)}) collective-permute-start(bf16[8,128,128]{2,1,0:T(8,128)(2,1)S(1)} %collective-permute-done.1.refs_0_.refs_4_), channel_id=1, source_target_pairs={{0,2},{2,4},{4,6},{6,8},{8,10},{10,12},{12,14},{14,0},{1,3},{3,5},... | collective-permute-start | bytes 786440 | tf_op jit(solution)/shard_map/ppermute | solution.py:188
  36.1 11.2 %collective-permute-start.4 = (bf16[8,128,128]{2,1,0:T(8,128)(2,1)S(1)}, bf16[8,128,128]{2,1,0:T(8,128)(2,1)S(1)}, u32[]{:S(2)}, u32[]{:S(2)}) collective-permute-start(bf16[8,128,128]{2,1,0:T(8,128)(2,1)S(1)} %collective-permute-done.2.refs_1_.refs_5_), channel_id=1, source_target_pairs={{0,14},{2,0},{4,2},{6,4},{8,6},{10,8},{12,10},{14,12},{1,15},{3,1}... | collective-permute-start | bytes 786440 | tf_op jit(solution)/shard_map/ppermute | solution.py:188
  41.7 10.5 %collective-permute-start.10 = (bf16[8,128,128]{2,1,0:T(8,128)(2,1)S(1)}, bf16[8,128,128]{2,1,0:T(8,128)(2,1)S(1)}, u32[]{:S(2)}, u32[]{:S(2)}) collective-permute-start(bf16[8,128,128]{2,1,0:T(8,128)(2,1)S(1)} %collective-permute-done.6.refs_1_.refs_7_), channel_id=1, source_target_pairs={{0,14},{2,0},{4,2},{6,4},{8,6},{10,8},{12,10},{14,12},{1,15},{3,1}... | collective-permute-start | bytes 786440 | tf_op jit(solution)/shard_map/ppermute | solution.py:188
  44.3 8.0 %collective-permute-start.9 = (bf16[8,128,128]{2,1,0:T(8,128)(2,1)S(1)}, bf16[8,128,128]{2,1,0:T(8,128)(2,1)S(1)}, u32[]{:S(2)}, u32[]{:S(2)}) collective-permute-start(bf16[8,128,128]{2,1,0:T(8,128)(2,1)S(1)} %collective-permute-done.5.refs_0_.refs_6_), channel_id=1, source_target_pairs={{0,2},{2,4},{4,6},{6,8},{8,10},{10,12},{12,14},{14,0},{1,3},{3,5},... | collective-permute-start | bytes 786440 | tf_op jit(solution)/shard_map/ppermute | solution.py:188
  47.3 10.4 %collective-permute-start.7 = (bf16[8,128,128]{2,1,0:T(8,128)(2,1)S(1)}, bf16[8,128,128]{2,1,0:T(8,128)(2,1)S(1)}, u32[]{:S(2)}, u32[]{:S(2)}) collective-permute-start(bf16[8,128,128]{2,1,0:T(8,128)(2,1)S(1)} %collective-permute-done.3.refs_0_.refs_8_), channel_id=1, source_target_pairs={{0,2},{2,4},{4,6},{6,8},{8,10},{10,12},{12,14},{14,0},{1,3},{3,5},... | collective-permute-start | bytes 786440 | tf_op jit(solution)/shard_map/ppermute | solution.py:188
  47.3 10.4 %collective-permute-start.8 = (bf16[8,128,128]{2,1,0:T(8,128)(2,1)S(1)}, bf16[8,128,128]{2,1,0:T(8,128)(2,1)S(1)}, u32[]{:S(2)}, u32[]{:S(2)}) collective-permute-start(bf16[8,128,128]{2,1,0:T(8,128)(2,1)S(1)} %collective-permute-done.4.refs_1_.refs_9_), channel_id=1, source_target_pairs={{0,14},{2,0},{4,2},{6,4},{8,6},{10,8},{12,10},{14,12},{1,15},{3,1}... | collective-permute-start | bytes 786440 | tf_op jit(solution)/shard_map/ppermute | solution.py:188
  52.2 11.1 %collective-permute-start.13 = (bf16[8,128,128]{2,1,0:T(8,128)(2,1)S(1)}, bf16[8,128,128]{2,1,0:T(8,128)(2,1)S(1)}, u32[]{:S(2)}, u32[]{:S(2)}) collective-permute-start(bf16[8,128,128]{2,1,0:T(8,128)(2,1)S(1)} %collective-permute-done.9.refs_0_.refs_10_), channel_id=1, source_target_pairs={{0,2},{2,4},{4,6},{6,8},{8,10},{10,12},{12,14},{14,0},{1,3},{3,5},... | collective-permute-start | bytes 786440 | tf_op jit(solution)/shard_map/ppermute | solution.py:188
  52.3 11.0 %collective-permute-start.14 = (bf16[8,128,128]{2,1,0:T(8,128)(2,1)S(1)}, bf16[8,128,128]{2,1,0:T(8,128)(2,1)S(1)}, u32[]{:S(2)}, u32[]{:S(2)}) collective-permute-start(bf16[8,128,128]{2,1,0:T(8,128)(2,1)S(1)} %collective-permute-done.10.refs_1_.refs_11_), channel_id=1, source_target_pairs={{0,14},{2,0},{4,2},{6,4},{8,6},{10,8},{12,10},{14,12},{1,15},{3,1}... | collective-permute-start | bytes 786440 | tf_op jit(solution)/shard_map/ppermute | solution.py:188
  57.7 10.9 %collective-permute-start.11 = (bf16[8,128,128]{2,1,0:T(8,128)(2,1)S(1)}, bf16[8,128,128]{2,1,0:T(8,128)(2,1)S(1)}, u32[]{:S(2)}, u32[]{:S(2)}) collective-permute-start(bf16[8,128,128]{2,1,0:T(8,128)(2,1)S(1)} %collective-permute-done.7.refs_0_.refs_12_), channel_id=1, source_target_pairs={{0,2},{2,4},{4,6},{6,8},{8,10},{10,12},{12,14},{14,0},{1,3},{3,5},... | collective-permute-start | bytes 786440 | tf_op jit(solution)/shard_map/ppermute | solution.py:188
  57.8 10.8 %collective-permute-start.12 = (bf16[8,128,128]{2,1,0:T(8,128)(2,1)S(1)}, bf16[8,128,128]{2,1,0:T(8,128)(2,1)S(1)}, u32[]{:S(2)}, u32[]{:S(2)}) collective-permute-start(bf16[8,128,128]{2,1,0:T(8,128)(2,1)S(1)} %collective-permute-done.8.refs_1_.refs_13_), channel_id=1, source_target_pairs={{0,14},{2,0},{4,2},{6,4},{8,6},{10,8},{12,10},{14,12},{1,15},{3,1}... | collective-permute-start | bytes 786440 | tf_op jit(solution)/shard_map/ppermute | solution.py:188
  69.9 3.8 collective-permute-start.15
  72.4 1.3 collective-permute-start.16
